TPU v7x, 256 devices: a whole 4x4x8 slice. The times are simulated.
256 devices in a mesh: seq: 64 (over y, z, core), head: 4 (over x).
Axes of the slice: x: 4, y: 4, z: 8, core: 2. Of those that a mesh axis runs over, the one named last changes fastest.
Arguments:
- tokens: bfloat16 [16384, 2048], P('seq')
- w_qkv: bfloat16 [2048, 3, 2048], P(None, None, 'head'), may hold values from -0.125 to 0.125
- w_out: bfloat16 [2048, 2048], P('head'), may hold values from -0.125 to 0.125
- norm_gain: float32 [2048], replicated, may hold values from 0.25 to 1.75
- w_label: bfloat16 [2048, 128], replicated, may hold values from -0.125 to 0.125
- offset_mid: int32 [16], P('head'), may hold values from 0 to 7
- offset_far: int32 [16], P('head'), may hold values from 0 to 63
Outputs:
- logits: float32 [16384, 128], P('seq')
All inputs are finite; a program needn't handle non-finite values.
Results may differ from a plain program's by a relative error of at most 0.023.
The roundings to bfloat16 on the way count: a program that leaves them out, or rounds other values in their place, can miss the bound.
Values may be sent and summed in bfloat16 or wider, within the bound.
No kernel may reach another device: no remote copies, remote signals or barrier semaphores. Data moves between devices by JAX's collectives and lax.ppermute only.
A program may use at most 64 MiB of HBM per device.

v0:
```python
import jax
import jax.numpy as jnp
from jax import lax
from jax.sharding import PartitionSpec as P

SPAN = 8


def from_behind(block, axis, distance):
    devices = range(lax.axis_size(axis))
    route = [((i - distance) % len(devices), i) for i in devices]
    return lax.ppermute(block, axis, route)


def attend(queries, keys, values):
    scores = jnp.einsum(
        "rhe,she->hrs", queries, keys, preferred_element_type=jnp.float32
    ) / jnp.sqrt(jnp.float32(queries.shape[2]))
    top = jnp.max(scores, axis=-1)
    weights = jnp.exp(scores - top[..., None])
    total = jnp.sum(weights, axis=-1)
    summed = jnp.einsum(
        "hrs,she->rhe", weights.astype(jnp.bfloat16), values, preferred_element_type=jnp.float32
    )
    return (top.T, total.T, summed)


def select_rows(array, offsets, rate):
    rows = array.shape[0] // rate
    shaped = array.reshape(rows, rate, array.shape[1], array.shape[2])
    index = jnp.broadcast_to(
        offsets[None, None, :, None], (rows, 1, array.shape[1], array.shape[2])
    )
    return jnp.take_along_axis(shaped, index, axis=1)[:, 0]


def spread_rows(parts, offsets, rate):
    top, total, summed = parts
    rows = top.shape[0]
    marks = jnp.arange(rate, dtype=jnp.int32)[None, :, None] == offsets[None, None, :]
    top_full = jnp.where(marks, top[:, None, :], jnp.float32(-1e30)).reshape(rows * rate, -1)
    total_full = jnp.where(marks, total[:, None, :], jnp.float32(0.0)).reshape(rows * rate, -1)
    sum_full = jnp.where(marks[..., None], summed[:, None], jnp.float32(0.0)).reshape(
        rows * rate, summed.shape[1], summed.shape[2]
    )
    return (top_full, total_full, sum_full)


def body(tokens, w_qkv, w_out, norm_gain, w_label, offset_mid, offset_far):
    tok_rows = tokens.shape[0]
    local_heads = offset_mid.shape[0]
    head_size = w_qkv.shape[2] // local_heads
    qkv = jnp.einsum("td,dce->tce", tokens, w_qkv, preferred_element_type=jnp.float32).astype(
        jnp.bfloat16
    )
    qkv = qkv.reshape(tok_rows, 3, local_heads, head_size)
    queries, keys, values = (qkv[:, 0], qkv[:, 1], qkv[:, 2])
    seq_count = lax.axis_size("seq")
    near = attend(queries, keys, values)
    mid_q = select_rows(queries, offset_mid, SPAN)
    mid_kv = jnp.stack(
        [select_rows(keys, offset_mid, SPAN), select_rows(values, offset_mid, SPAN)], axis=0
    )
    mid_rows = mid_kv.shape[1]
    position = (lax.axis_index("seq") + SPAN // 2) % SPAN
    lower_pieces = []
    upper_pieces = []
    for step_back in range(1, SPAN):
        lower_pieces.insert(0, from_behind(mid_kv, "seq", step_back))
        upper_pieces.append(from_behind(mid_kv, "seq", -step_back))
    window = jnp.concatenate(lower_pieces + [mid_kv] + upper_pieces, axis=1)
    gathered = lax.dynamic_slice_in_dim(
        window, (SPAN - 1 - position) * mid_rows, SPAN * mid_rows, 1
    )
    middle = spread_rows(attend(mid_q, gathered[0], gathered[1]), offset_mid, SPAN)
    far_q = select_rows(queries, offset_far, seq_count)
    far_kv = jnp.stack(
        [select_rows(keys, offset_far, seq_count), select_rows(values, offset_far, seq_count)],
        axis=0,
    )
    far_all = lax.all_gather(far_kv, "seq", axis=1, tiled=True)
    distant = spread_rows(attend(far_q, far_all[0], far_all[1]), offset_far, seq_count)
    branches = [near, middle, distant]
    peak = jnp.maximum(jnp.maximum(near[0], middle[0]), distant[0])
    upper = jnp.zeros((tok_rows, local_heads, head_size), jnp.float32)
    lower = jnp.zeros((tok_rows, local_heads), jnp.float32)
    for top, total, summed in branches:
        factor = jnp.exp(top - peak)
        upper = upper + factor[..., None] * summed
        lower = lower + factor * total
    attn = (
        (upper / lower[..., None]).astype(jnp.bfloat16).reshape(tok_rows, local_heads * head_size)
    )
    partial_out = jnp.dot(attn, w_out, preferred_element_type=jnp.float32)
    projected = lax.psum(partial_out.astype(jnp.bfloat16), "head").astype(jnp.float32)
    mixed = tokens.astype(jnp.float32) + projected
    mean_sq = jnp.mean(mixed * mixed, axis=-1)
    scaled = (mixed * norm_gain).astype(jnp.bfloat16)
    product = jnp.dot(scaled, w_label, preferred_element_type=jnp.float32)
    return product / jnp.sqrt(mean_sq + 1e-05)[:, None]


def solution(mesh):
    return jax.shard_map(
        body,
        mesh=mesh,
        in_specs=(
            P("seq", None),
            P(None, None, "head"),
            P("head", None),
            P(),
            P(),
            P("head"),
            P("head"),
        ),
        out_specs=P("seq", None),
        check_vma=False,
    )
```

profile of v0, /device:TPU:8, one launch (start us, length us, event | category | flops | bytes accessed | tf_op | source)
XLA Modules:
  0.0 969.6 jit_solution(3699433661671569265)
XLA Ops:
  6.5 5.9 convolution_convert_fusion.1
  12.5 1.7 reshape.163
  14.2 1.0 fusion.55
  16.3 235.5 %gather_fusion.1 = bf16[16384]{0:T(1024)(128)(2,1)} fusion(bf16[32,8,4,128]{3,1,0,2:T(8,128)(2,1)S(1)} %get-tuple-element.34, s32[16384]{0:T(1024)S(1)} %bitcast.149), kind=kCustom, calls=%fused_computation.2.clone | custom fusion | bytes 327680 | tf_op jit(solution)/shard_map/jit(take_along_axis)/gather | solution.py:34
  251.7 236.4 %gather_fusion.2 = bf16[16384]{0:T(1024)(128)(2,1)} fusion(bf16[32,8,4,128]{3,1,0,2:T(8,128)(2,1)S(1)} %get-tuple-element.20, s32[16384]{0:T(1024)S(1)} %bitcast.150), kind=kCustom, calls=%fused_computation.3.clone | custom fusion | bytes 327680 | tf_op jit(solution)/shard_map/jit(take_along_axis)/gather | solution.py:34
  488.1 0.9 fusion.28
  489.6 4.1 collective-permute-start
  493.6 4.0 collective-permute-start.1
  498.0 3.2 collective-permute-start.3
  501.2 2.6 collective-permute-start.4
  503.8 2.2 fusion.59
  507.2 0.9 copy.77
  508.1 236.0 %gather_fusion = bf16[16384]{0:T(1024)(128)(2,1)} fusion(bf16[32,8,4,128]{3,1,0,2:T(8,128)(2,1)S(1)} %bitcast.152, s32[16384]{0:T(1024)S(1)} %bitcast.151), kind=kCustom, calls=%fused_computation.clone | custom fusion | bytes 327680 | tf_op jit(solution)/shard_map/jit(take_along_axis)/gather | solution.py:34
  744.2 22.2 %gather_fusion.5 = bf16[2048]{0:T(1024)(128)(2,1)S(1)} fusion(bf16[4,64,4,128]{3,1,0,2:T(8,128)(2,1)S(1)} %bitcast.158, s32[2048]{0:T(1024)S(1)} %bitcast.154), kind=kCustom, calls=%fused_computation.5.clone | custom fusion | bytes 40960 | tf_op jit(solution)/shard_map/jit(take_along_axis)/gather | solution.py:34
  766.4 22.2 %gather_fusion.4 = bf16[2048]{0:T(1024)(128)(2,1)S(1)} fusion(bf16[4,64,4,128]{3,1,0,2:T(8,128)(2,1)S(1)} %bitcast.157, s32[2048]{0:T(1024)S(1)} %bitcast.155), kind=kCustom, calls=%fused_computation.4.clone | custom fusion | bytes 40960 | tf_op jit(solution)/shard_map/jit(take_along_axis)/gather | solution.py:34
  788.6 22.2 %gather_fusion.3 = bf16[2048]{0:T(1024)(128)(2,1)S(1)} fusion(bf16[4,64,4,128]{3,1,0,2:T(8,128)(2,1)S(1)} %bitcast.153, s32[2048]{0:T(1024)S(1)} %bitcast.156), kind=kCustom, calls=%fused_computation.1.clone | custom fusion | bytes 40960 | tf_op jit(solution)/shard_map/jit(take_along_axis)/gather | solution.py:34
  810.8 48.7 %all_gather.3 = bf16[2,256,4,128]{3,2,0,1:T(4,128)(2,1)S(1)} all-gather(bf16[2,4,4,128]{3,2,0,1:T(4,128)(2,1)S(1)} %copy.67), channel_id=1, replica_groups=mesh['seq'=64,'head'=4] {'seq'}, dimensions={1}, use_global_device_ids=true | all-gather | bytes 532480 | tf_op jit(solution)/shard_map/all_gather | solution.py:81
  860.9 0.6 broadcast_in_dim.167
  861.5 0.7 broadcast_in_dim.168
  862.2 0.7 broadcast_in_dim.173
  862.9 0.7 broadcast_in_dim.174
  863.5 0.8 broadcast_in_dim.183
  864.4 2.0 copy.73
  866.4 1.3 collective-permute-start.5
  867.7 0.8 constant_dynamic-update-slice_fusion.14
  868.6 0.9 constant_dynamic-update-slice_fusion.13
  869.5 3.9 collective-permute-start.7
  873.4 0.9 constant_dynamic-update-slice_fusion.12
  874.2 0.8 collective-permute-start.8
  875.1 0.9 constant_dynamic-update-slice_fusion.11
  876.0 0.9 constant_dynamic-update-slice_fusion.10
  876.9 1.3 collective-permute-start.10
  878.2 1.7 collective-permute-start.11
  879.9 5.6 collective-permute-start.12
  885.5 0.8 collective-permute-start.13
  886.8 1.1 collective-permute-done.11
  887.9 6.6 collective-permute-done.12
  894.6 0.9 copy-done.5
  895.6 1.1 fusion.58
  897.2 1.2 convolution_bitcast_fusion.1
  898.4 0.9 broadcast_bitcast_fusion
  899.2 2.0 copy.71
  901.3 0.7 fusion.43
  902.0 1.6 fusion.4
  903.6 1.7 convolution_convert_fusion
  905.4 52.9 %all-reduce.2.cloned.1.call-done = bf16[256,2048]{1,0:T(8,128)(2,1)} async-done(((bf16[256,2048]{1,0:T(8,128)(2,1)}), bf16[256,2048]{1,0:T(8,128)(2,1)}) %all-reduce.2.cloned.1.call-update) | async-done | bytes 1048592 | tf_op jit(solution)/shard_map/psum | solution.py:95
  958.2 2.0 multiply_reduce_fusion
  960.2 2.5 convolution_divide_fusion
  (89 shorter events, 6.2 us)
Async XLA Ops:
  6.5 897.1 %copy-start = (bf16[512,2048]{1,0:T(8,128)(2,1)S(1)}, bf16[512,2048]{1,0:T(8,128)(2,1)}, u32[]{:S(2)}) copy-start(bf16[512,2048]{1,0:T(8,128)(2,1)} %param.13) | copy-start | bytes 6291460
  6.5 8.7 copy-start.6
  6.5 8.7 copy-start.9
  6.5 951.7 %all-reduce.2.cloned.1.call-start = ((), (), s32[]{:S(2)}) async-start(), calls=%async_computation | async-start | bytes 2097152 | tf_op jit(solution)/shard_map/psum | solution.py:95
  15.2 0.8 copy-start.3
  15.2 472.9 %copy-start.8 = (s32[4]{0:T(128)}, s32[4]{0:T(128)S(1)}, u32[]{:S(2)}) copy-start(s32[4]{0:T(128)S(1)} %broadcast_add_fusion.1) | copy-start | bytes 52
  15.8 472.3 %copy-start.7 = (pred[4]{0:T(512)(128)(4,1)}, pred[4]{0:T(512)(128)(4,1)S(1)}, u32[]{:S(2)}) copy-start(pred[4]{0:T(512)(128)(4,1)S(1)} %get-tuple-element.36) | copy-start | bytes 16
  251.7 252.0 %copy-start.2 = (bf16[256,1,4,128]{3,2,0,1:T(4,128)(2,1)S(1)}, bf16[256,1,4,128]{3,2,0,1:T(4,128)(2,1)}, u32[]{:S(2)}) copy-start(bf16[256,1,4,128]{3,2,0,1:T(4,128)(2,1)} %get-tuple-element.12) | copy-start | bytes 786436
  489.6 376.8 %collective-permute-start = (bf16[2,32,4,128]{3,1,2,0:T(8,128)(2,1)}, bf16[2,32,4,128]{3,1,2,0:T(8,128)(2,1)}, u32[]{:S(2)}, u32[]{:S(2)}) collective-permute-start(bf16[2,32,4,128]{3,1,2,0:T(8,128)(2,1)} %pad_maximum_fusion), channel_id=1, source_target_pairs={{228,0},{232,4},{236,8},{240,12},{244,16},{248,20},{252,24},{0,28}... | collective-permute-start | bytes 196616 | tf_op jit(solution)/shard_map/ppermute | solution.py:12
  493.6 374.9 %collective-permute-start.1 = (bf16[2,32,4,128]{3,1,2,0:T(8,128)(2,1)}, bf16[2,32,4,128]{3,1,2,0:T(8,128)(2,1)}, u32[]{:S(2)}, u32[]{:S(2)}) collective-permute-start(bf16[2,32,4,128]{3,1,2,0:T(8,128)(2,1)} %pad_maximum_fusion), channel_id=1, source_target_pairs={{232,0},{236,4},{240,8},{244,12},{248,16},{252,20},{0,24},{4,28},{... | collective-permute-start | bytes 196616 | tf_op jit(solution)/shard_map/ppermute | solution.py:12
  497.7 371.8 %collective-permute-start.2 = (bf16[2,32,4,128]{3,1,2,0:T(8,128)(2,1)}, bf16[2,32,4,128]{3,1,2,0:T(8,128)(2,1)}, u32[]{:S(2)}, u32[]{:S(2)}) collective-permute-start(bf16[2,32,4,128]{3,1,2,0:T(8,128)(2,1)} %pad_maximum_fusion), channel_id=1, source_target_pairs={{236,0},{240,4},{244,8},{248,12},{252,16},{0,20},{4,24},{8,28},{12... | collective-permute-start | bytes 196616 | tf_op jit(solution)/shard_map/ppermute | solution.py:12
  498.0 376.3 %collective-permute-start.3 = (bf16[2,32,4,128]{3,1,2,0:T(8,128)(2,1)}, bf16[2,32,4,128]{3,1,2,0:T(8,128)(2,1)}, u32[]{:S(2)}, u32[]{:S(2)}) collective-permute-start(bf16[2,32,4,128]{3,1,2,0:T(8,128)(2,1)} %pad_maximum_fusion), channel_id=1, source_target_pairs={{240,0},{244,4},{248,8},{252,12},{0,16},{4,20},{8,24},{12,28},{16,... | collective-permute-start | bytes 196616 | tf_op jit(solution)/shard_map/ppermute | solution.py:12
  501.2 374.8 %collective-permute-start.4 = (bf16[2,32,4,128]{3,1,2,0:T(8,128)(2,1)}, bf16[2,32,4,128]{3,1,2,0:T(8,128)(2,1)}, u32[]{:S(2)}, u32[]{:S(2)}) collective-permute-start(bf16[2,32,4,128]{3,1,2,0:T(8,128)(2,1)} %pad_maximum_fusion), channel_id=1, source_target_pairs={{244,0},{248,4},{252,8},{0,12},{4,16},{8,20},{12,24},{16,28},{20,3... | collective-permute-start | bytes 196616 | tf_op jit(solution)/shard_map/ppermute | solution.py:12
  508.1 236.0 %copy-start.10 = (pred[4]{0:T(512)(128)(4,1)S(1)}, pred[4]{0:T(512)(128)(4,1)}, u32[]{:S(2)}) copy-start(pred[4]{0:T(512)(128)(4,1)} %get-tuple-element.35) | copy-start | bytes 16
  788.6 71.4 %copy-start.1 = (f32[4,256,256]{1,2,0:T(8,128)S(1)}, f32[4,256,256]{1,2,0:T(8,128)}, u32[]{:S(2)}) copy-start(f32[4,256,256]{1,2,0:T(8,128)} %get-tuple-element.32) | copy-start | bytes 3145732
  866.4 10.5 %collective-permute-start.5 = (bf16[2,32,4,128]{3,1,2,0:T(8,128)(2,1)}, bf16[2,32,4,128]{3,1,2,0:T(8,128)(2,1)S(1)}, u32[]{:S(2)}, u32[]{:S(2)}) collective-permute-start(bf16[2,32,4,128]{3,1,2,0:T(8,128)(2,1)} %pad_maximum_fusion), channel_id=1, source_target_pairs={{248,0},{252,4},{0,8},{4,12},{8,16},{12,20},{16,24},{20,28},{24,32... | collective-permute-start | bytes 196616 | tf_op jit(solution)/shard_map/ppermute | solution.py:12
  868.5 9.7 collective-permute-start.6
  869.5 10.4 %collective-permute-start.7 = (bf16[2,32,4,128]{3,1,2,0:T(8,128)(2,1)}, bf16[2,32,4,128]{3,1,2,0:T(8,128)(2,1)S(1)}, u32[]{:S(2)}, u32[]{:S(2)}) collective-permute-start(bf16[2,32,4,128]{3,1,2,0:T(8,128)(2,1)} %pad_maximum_fusion), channel_id=1, source_target_pairs={{4,0},{8,4},{12,8},{16,12},{20,16},{24,20},{28,24},{32,28},{36,32}... | collective-permute-start | bytes 196616 | tf_op jit(solution)/shard_map/ppermute | solution.py:12
  874.2 11.2 %collective-permute-start.8 = (bf16[2,32,4,128]{3,1,2,0:T(8,128)(2,1)}, bf16[2,32,4,128]{3,1,2,0:T(8,128)(2,1)S(1)}, u32[]{:S(2)}, u32[]{:S(2)}) collective-permute-start(bf16[2,32,4,128]{3,1,2,0:T(8,128)(2,1)} %pad_maximum_fusion), channel_id=1, source_target_pairs={{8,0},{12,4},{16,8},{20,12},{24,16},{28,20},{32,24},{36,28},{40,32... | collective-permute-start | bytes 196616 | tf_op jit(solution)/shard_map/ppermute | solution.py:12
  875.9 10.4 %collective-permute-start.9 = (bf16[2,32,4,128]{3,1,2,0:T(8,128)(2,1)}, bf16[2,32,4,128]{3,1,2,0:T(8,128)(2,1)S(1)}, u32[]{:S(2)}, u32[]{:S(2)}) collective-permute-start(bf16[2,32,4,128]{3,1,2,0:T(8,128)(2,1)} %pad_maximum_fusion), channel_id=1, source_target_pairs={{12,0},{16,4},{20,8},{24,12},{28,16},{32,20},{36,24},{40,28},{44,3... | collective-permute-start | bytes 196616 | tf_op jit(solution)/shard_map/ppermute | solution.py:12
  876.9 9.9 %collective-permute-start.10 = (bf16[2,32,4,128]{3,1,2,0:T(8,128)(2,1)}, bf16[2,32,4,128]{3,1,2,0:T(8,128)(2,1)S(1)}, u32[]{:S(2)}, u32[]{:S(2)}) collective-permute-start(bf16[2,32,4,128]{3,1,2,0:T(8,128)(2,1)} %pad_maximum_fusion), channel_id=1, source_target_pairs={{16,0},{20,4},{24,8},{28,12},{32,16},{36,20},{40,24},{44,28},{48,3... | collective-permute-start | bytes 196616 | tf_op jit(solution)/shard_map/ppermute | solution.py:12
  878.2 9.7 %collective-permute-start.11 = (bf16[2,32,4,128]{3,1,2,0:T(8,128)(2,1)}, bf16[2,32,4,128]{3,1,2,0:T(8,128)(2,1)S(1)}, u32[]{:S(2)}, u32[]{:S(2)}) collective-permute-start(bf16[2,32,4,128]{3,1,2,0:T(8,128)(2,1)} %pad_maximum_fusion), channel_id=1, source_target_pairs={{20,0},{24,4},{28,8},{32,12},{36,16},{40,20},{44,24},{48,28},{52,3... | collective-permute-start | bytes 196616 | tf_op jit(solution)/shard_map/ppermute | solution.py:12
  879.9 14.6 %collective-permute-start.12 = (bf16[2,32,4,128]{3,1,2,0:T(8,128)(2,1)}, bf16[2,32,4,128]{3,1,2,0:T(8,128)(2,1)S(1)}, u32[]{:S(2)}, u32[]{:S(2)}) collective-permute-start(bf16[2,32,4,128]{3,1,2,0:T(8,128)(2,1)} %pad_maximum_fusion), channel_id=1, source_target_pairs={{24,0},{28,4},{32,8},{36,12},{40,16},{44,20},{48,24},{52,28},{56,3... | collective-permute-start | bytes 196616 | tf_op jit(solution)/shard_map/ppermute | solution.py:12
  885.5 9.1 collective-permute-start.13
  894.6 1.0 copy-start.5
  897.1 63.1 %copy-start.11 = (f32[2048]{0:T(1024)S(1)}, f32[2048]{0:T(1024)}, u32[]{:S(2)}) copy-start(f32[2048]{0:T(1024)} %param.14) | copy-start | bytes 24580
  903.6 56.6 %copy-start.4 = (bf16[256,2048]{1,0:T(8,128)(2,1)S(1)}, bf16[256,2048]{1,0:T(8,128)(2,1)}, u32[]{:S(2)}) copy-start(bf16[256,2048]{1,0:T(8,128)(2,1)} %param.11) | copy-start | bytes 3145732
Sparse Core Ops, SparseCore 0:
  905.5 52.6 all-reduce.1
where the time goes:
time: 970 us
  local copies, waits for them, and re-layouts  793 us (82%)
  waiting for transfers between devices  61.1 us (6%)
  blocking collectives  48.7 us (5%)
  starting transfers between devices  29.6 us (3%)
  matrix products  16.8 us (2%)
  between operations  13.7 us (1%)
    gather x7, local copies, waits for them, and re-layouts, select_rows(): return jnp.take_along_axis(shaped, index, axis=1)[:, 0]  774 us
    psum x1, waiting for transfers between devices, body(): lax.psum(partial_out.astype(jnp.bfloat16), 'head').astype(jnp.float32)  52.9 us
    all_gather x1, blocking collectives, body(): far_all = lax.all_gather(far_kv, 'seq', axis=1, tiled=True)  48.7 us
    ppermute x14, starting transfers between devices, from_behind(): return lax.ppermute(block, axis, route)  29.6 us
  transfers between devices with their start and end apart: 15, of which 5 were waited for; matrix products, arithmetic and copies ran while one was open for 33% of the time, Pallas kernels for 0%

commit v1 on v0

--- a/solution.py
+++ b/solution.py
@@ -92,7 +92,9 @@
         (upper / lower[..., None]).astype(jnp.bfloat16).reshape(tok_rows, local_heads * head_size)
     )
     partial_out = jnp.dot(attn, w_out, preferred_element_type=jnp.float32)
-    projected = lax.psum(partial_out.astype(jnp.bfloat16), "head").astype(jnp.float32)
+    projected = jnp.sum(lax.all_gather(partial_out.astype(jnp.bfloat16), "head"), axis=0).astype(
+        jnp.float32
+    )
     mixed = tokens.astype(jnp.float32) + projected
     mean_sq = jnp.mean(mixed * mixed, axis=-1)
     scaled = (mixed * norm_gain).astype(jnp.bfloat16)

time: 970 us -> 952 us (0.981)
  local copies, waits for them, and re-layouts: 793 us -> 722 us
  waiting for transfers between devices: 61.1 us -> 115 us
  starting transfers between devices: 29.6 us -> 18.5 us
    gather x7, local copies, waits for them, and re-layouts: 774 us -> 702 us  [select_rows(): return jnp.take_along_axis(shaped, index, axis=1)[:, 0]]
    all_gather x0 -> x1, waiting for transfers between devices: none -> 62.3 us  [body(): lax.all_gather(partial_out.astype(jnp.bfloat16), 'head')]
    psum x1 -> x0, waiting for transfers between devices: 52.9 us -> none  [body(): lax.psum(partial_out.astype(jnp.bfloat16), 'head').astype(jnp.float32)]
    ppermute x14, waiting for transfers between devices: 8.24 us -> 52.9 us  [from_behind(): return lax.ppermute(block, axis, route)]
    ppermute x14, starting transfers between devices: 29.6 us -> 18.5 us  [from_behind(): return lax.ppermute(block, axis, route)]
  transfers between devices with their start and end apart: 15 -> 15, of which waited for: 5 -> 10; matrix products, arithmetic and copies ran while one was open for 33% -> 26% of each run, Pallas kernels for 0% -> 0%
where the time goes in v1:
time: 952 us; the launch traced here: 950 us
  local copies, waits for them, and re-layouts  722 us (76%)
  waiting for transfers between devices  115 us (12%)
  blocking collectives  51 us (5%)
  starting transfers between devices  18.5 us (2%)
  matrix products  16.5 us (2%)
  other arithmetic  13.7 us (1%)
  between operations  13.7 us (1%)
    gather x7, local copies, waits for them, and re-layouts, select_rows(): return jnp.take_along_axis(shaped, index, axis=1)[:, 0]  702 us
    all_gather x1, waiting for transfers between devices, body(): lax.all_gather(partial_out.astype(jnp.bfloat16), 'head')  62.3 us
    ppermute x14, waiting for transfers between devices, from_behind(): return lax.ppermute(block, axis, route)  52.9 us
    all_gather x1, blocking collectives, body(): far_all = lax.all_gather(far_kv, 'seq', axis=1, tiled=True)  51 us
  transfers between devices with their start and end apart: 15, of which 10 were waited for; matrix products, arithmetic and copies ran while one was open for 26% of the time, Pallas kernels for 0%

profile of v1, /device:TPU:8, one launch (start us, length us, event | category | flops | bytes accessed | tf_op | source)
XLA Modules:
  0.0 950.5 jit_solution(2401612704691737347)
XLA Ops:
  6.5 0.8 broadcast_add_fusion.1
  7.3 1.3 broadcast_compare_fusion
  9.5 5.8 convolution_convert_fusion.1
  15.3 1.7 reshape.163
  17.1 1.0 fusion.55
  18.9 235.9 %gather_fusion.2 = bf16[16384]{0:T(1024)(128)(2,1)} fusion(bf16[32,8,4,128]{3,1,0,2:T(8,128)(2,1)S(1)} %get-tuple-element.20, s32[16384]{0:T(1024)S(1)} %bitcast.150), kind=kCustom, calls=%fused_computation.3.clone | custom fusion | bytes 327680 | tf_op jit(solution)/shard_map/jit(take_along_axis)/gather | solution.py:34
  254.9 235.5 %gather_fusion.1 = bf16[16384]{0:T(1024)(128)(2,1)} fusion(bf16[32,8,4,128]{3,1,0,2:T(8,128)(2,1)S(1)} %get-tuple-element.34, s32[16384]{0:T(1024)S(1)} %bitcast.151), kind=kCustom, calls=%fused_computation.2.clone | custom fusion | bytes 327680 | tf_op jit(solution)/shard_map/jit(take_along_axis)/gather | solution.py:34
  490.3 0.9 fusion.28
  491.8 6.5 collective-permute-start.13
  498.5 6.9 collective-permute-start.11
  505.4 1.5 collective-permute-start.10
  507.6 0.9 copy.77
  508.6 2.2 fusion.59
  513.6 163.7 %gather_fusion = bf16[16384]{0:T(1024)(128)(2,1)S(1)} fusion(bf16[32,8,4,128]{3,1,0,2:T(8,128)(2,1)S(1)} %bitcast.153, s32[16384]{0:T(1024)S(1)} %bitcast.152), kind=kCustom, calls=%fused_computation.clone | custom fusion | bytes 327680 | tf_op jit(solution)/shard_map/jit(take_along_axis)/gather | solution.py:34
  677.3 22.2 %gather_fusion.3 = bf16[2048]{0:T(1024)(128)(2,1)S(1)} fusion(bf16[4,64,4,128]{3,1,0,2:T(8,128)(2,1)S(1)} %bitcast.154, s32[2048]{0:T(1024)S(1)} %bitcast.155), kind=kCustom, calls=%fused_computation.1.clone | custom fusion | bytes 40960 | tf_op jit(solution)/shard_map/jit(take_along_axis)/gather | solution.py:34
  699.5 22.2 %gather_fusion.5 = bf16[2048]{0:T(1024)(128)(2,1)S(1)} fusion(bf16[4,64,4,128]{3,1,0,2:T(8,128)(2,1)S(1)} %bitcast.159, s32[2048]{0:T(1024)S(1)} %bitcast.156), kind=kCustom, calls=%fused_computation.5.clone | custom fusion | bytes 40960 | tf_op jit(solution)/shard_map/jit(take_along_axis)/gather | solution.py:34
  721.6 22.2 %gather_fusion.4 = bf16[2048]{0:T(1024)(128)(2,1)S(1)} fusion(bf16[4,64,4,128]{3,1,0,2:T(8,128)(2,1)S(1)} %bitcast.158, s32[2048]{0:T(1024)S(1)} %bitcast.157), kind=kCustom, calls=%fused_computation.4.clone | custom fusion | bytes 40960 | tf_op jit(solution)/shard_map/jit(take_along_axis)/gather | solution.py:34
  743.9 51.0 %all_gather.9 = bf16[2,256,4,128]{3,2,0,1:T(4,128)(2,1)S(1)} all-gather(bf16[2,4,4,128]{3,2,0,1:T(4,128)(2,1)S(1)} %copy.67), channel_id=1, replica_groups=mesh['seq'=64,'head'=4] {'seq'}, dimensions={1}, use_global_device_ids=true | all-gather | bytes 532480 | tf_op jit(solution)/shard_map/all_gather | solution.py:81
  795.0 0.9 fusion.56
  796.3 1.2 convolution_bitcast_fusion.2
  797.4 1.4 fusion.7
  799.2 0.9 broadcast_in_dim.183
  800.0 2.1 copy.73
  802.1 1.1 collective-permute-start.1
  803.2 0.8 constant_dynamic-update-slice_fusion.14
  804.0 8.9 collective-permute-done.1
  812.9 8.2 collective-permute-done.2
  821.1 7.5 collective-permute-done.3
  828.6 6.9 collective-permute-done.4
  835.5 6.6 collective-permute-done.5
  842.1 6.0 collective-permute-done.6
  848.1 2.2 collective-permute-done.7
  850.3 4.5 collective-permute-done.8
  854.8 2.4 collective-permute-start.9
  857.2 2.2 collective-permute-done.9
  859.4 0.9 constant_dynamic-update-slice_fusion.3
  860.3 0.9 constant_dynamic-update-slice_fusion.2
  861.1 0.9 constant_dynamic-update-slice_fusion.1
  862.0 0.9 constant_dynamic-update-slice_fusion
  862.9 1.0 fusion.58
  867.1 0.9 broadcast_bitcast_fusion
  868.0 2.1 copy.71
  870.8 1.6 fusion.4
  872.4 1.7 convolution_convert_fusion
  874.1 62.3 %all-gather.3.cloned.1.call-done = bf16[1024,2048]{1,0:T(8,128)(2,1)} async-done(((bf16[256,2048]{1,0:T(8,128)(2,1)}), bf16[1024,2048]{1,0:T(8,128)(2,1)}) %all-gather.3.cloned.1.call-update) | async-done | bytes 4194320 | tf_op jit(solution)/shard_map/all_gather | solution.py:95
  936.4 3.1 reduce_sum.51
  939.5 1.6 multiply_reduce_fusion
  941.1 2.5 convolution_divide_fusion
  (92 shorter events, 11.1 us)
Async XLA Ops:
  6.5 865.8 %copy-start = (bf16[512,2048]{1,0:T(8,128)(2,1)S(1)}, bf16[512,2048]{1,0:T(8,128)(2,1)}, u32[]{:S(2)}) copy-start(bf16[512,2048]{1,0:T(8,128)(2,1)} %param.13) | copy-start | bytes 6291460
  6.5 929.8 %all-gather.3.cloned.1.call-start = ((), (), s32[]{:S(2)}) async-start(), calls=%async_computation | async-start | bytes 5242880 | tf_op jit(solution)/shard_map/all_gather | solution.py:95
  7.3 483.0 %copy-start.9 = (s32[4]{0:T(128)}, s32[4]{0:T(128)S(1)}, u32[]{:S(2)}) copy-start(s32[4]{0:T(128)S(1)} %broadcast_add_fusion.1) | copy-start | bytes 52
  8.6 481.7 %copy-start.8 = (pred[4]{0:T(512)(128)(4,1)}, pred[4]{0:T(512)(128)(4,1)S(1)}, u32[]{:S(2)}) copy-start(pred[4]{0:T(512)(128)(4,1)S(1)} %get-tuple-element.36) | copy-start | bytes 16
  18.1 0.7 copy-start.3
  18.1 0.9 copy-start.5
  254.9 235.5 %copy-start.7 = (s32[4]{0:T(128)S(1)}, s32[4]{0:T(128)}, u32[]{:S(2)}) copy-start(s32[4]{0:T(128)} %param.16) | copy-start | bytes 52
  254.9 252.0 %copy-start.10 = (s32[4]{0:T(128)S(1)}, s32[4]{0:T(128)}, u32[]{:S(2)}) copy-start(s32[4]{0:T(128)} %param.17) | copy-start | bytes 52
  254.9 252.7 %copy-start.4 = (bf16[256,1,4,128]{3,2,0,1:T(4,128)(2,1)S(1)}, bf16[256,1,4,128]{3,2,0,1:T(4,128)(2,1)}, u32[]{:S(2)}) copy-start(bf16[256,1,4,128]{3,2,0,1:T(4,128)(2,1)} %copy-done.3) | copy-start | bytes 786436
  254.9 253.7 %copy-start.2 = (bf16[256,1,4,128]{3,2,0,1:T(4,128)(2,1)S(1)}, bf16[256,1,4,128]{3,2,0,1:T(4,128)(2,1)}, u32[]{:S(2)}) copy-start(bf16[256,1,4,128]{3,2,0,1:T(4,128)(2,1)} %get-tuple-element.12) | copy-start | bytes 786436
  491.8 370.2 %collective-permute-start.13 = (bf16[2,32,4,128]{3,1,2,0:T(8,128)(2,1)}, bf16[2,32,4,128]{3,1,2,0:T(8,128)(2,1)}, u32[]{:S(2)}, u32[]{:S(2)}) collective-permute-start(bf16[2,32,4,128]{3,1,2,0:T(8,128)(2,1)} %pad_maximum_fusion), channel_id=1, source_target_pairs={{28,0},{32,4},{36,8},{40,12},{44,16},{48,20},{52,24},{56,28},{60,3... | collective-permute-start | bytes 196616 | tf_op jit(solution)/shard_map/ppermute | solution.py:12
  498.4 362.8 %collective-permute-start.12 = (bf16[2,32,4,128]{3,1,2,0:T(8,128)(2,1)}, bf16[2,32,4,128]{3,1,2,0:T(8,128)(2,1)}, u32[]{:S(2)}, u32[]{:S(2)}) collective-permute-start(bf16[2,32,4,128]{3,1,2,0:T(8,128)(2,1)} %pad_maximum_fusion), channel_id=1, source_target_pairs={{24,0},{28,4},{32,8},{36,12},{40,16},{44,20},{48,24},{52,28},{56,3... | collective-permute-start | bytes 196616 | tf_op jit(solution)/shard_map/ppermute | solution.py:12
  498.5 361.8 %collective-permute-start.11 = (bf16[2,32,4,128]{3,1,2,0:T(8,128)(2,1)}, bf16[2,32,4,128]{3,1,2,0:T(8,128)(2,1)}, u32[]{:S(2)}, u32[]{:S(2)}) collective-permute-start(bf16[2,32,4,128]{3,1,2,0:T(8,128)(2,1)} %pad_maximum_fusion), channel_id=1, source_target_pairs={{20,0},{24,4},{28,8},{32,12},{36,16},{40,20},{44,24},{48,28},{52,3... | collective-permute-start | bytes 196616 | tf_op jit(solution)/shard_map/ppermute | solution.py:12
  505.4 354.0 %collective-permute-start.10 = (bf16[2,32,4,128]{3,1,2,0:T(8,128)(2,1)}, bf16[2,32,4,128]{3,1,2,0:T(8,128)(2,1)}, u32[]{:S(2)}, u32[]{:S(2)}) collective-permute-start(bf16[2,32,4,128]{3,1,2,0:T(8,128)(2,1)} %pad_maximum_fusion), channel_id=1, source_target_pairs={{16,0},{20,4},{24,8},{28,12},{32,16},{36,20},{40,24},{44,28},{48,3... | collective-permute-start | bytes 196616 | tf_op jit(solution)/shard_map/ppermute | solution.py:12
  506.9 295.2 %collective-permute-start = (bf16[2,32,4,128]{3,1,2,0:T(8,128)(2,1)}, bf16[2,32,4,128]{3,1,2,0:T(8,128)(2,1)}, u32[]{:S(2)}, u32[]{:S(2)}) collective-permute-start(bf16[2,32,4,128]{3,1,2,0:T(8,128)(2,1)} %pad_maximum_fusion), channel_id=1, source_target_pairs={{228,0},{232,4},{236,8},{240,12},{244,16},{248,20},{252,24},{0,28}... | collective-permute-start | bytes 196616 | tf_op jit(solution)/shard_map/ppermute | solution.py:12
  699.4 44.4 %copy-start.11 = (pred[4]{0:T(512)(128)(4,1)S(1)}, pred[4]{0:T(512)(128)(4,1)}, u32[]{:S(2)}) copy-start(pred[4]{0:T(512)(128)(4,1)} %get-tuple-element.35) | copy-start | bytes 16
  743.8 127.0 %copy-start.1 = (f32[4,256,256]{1,2,0:T(8,128)S(1)}, f32[4,256,256]{1,2,0:T(8,128)}, u32[]{:S(2)}) copy-start(f32[4,256,256]{1,2,0:T(8,128)} %get-tuple-element.32) | copy-start | bytes 3145732
  743.8 127.0 %copy-start.6 = (bf16[256,1,4,128]{0,3,2,1:T(8,128)(2,1)S(1)}, bf16[256,1,4,128]{0,3,2,1:T(8,128)(2,1)}, u32[]{:S(2)}) copy-start(bf16[256,1,4,128]{0,3,2,1:T(8,128)(2,1)} %copy.77) | copy-start | bytes 786436
  802.1 10.8 %collective-permute-start.1 = (bf16[2,32,4,128]{3,1,2,0:T(8,128)(2,1)}, bf16[2,32,4,128]{3,1,2,0:T(8,128)(2,1)S(1)}, u32[]{:S(2)}, u32[]{:S(2)}) collective-permute-start(bf16[2,32,4,128]{3,1,2,0:T(8,128)(2,1)} %pad_maximum_fusion), channel_id=1, source_target_pairs={{232,0},{236,4},{240,8},{244,12},{248,16},{252,20},{0,24},{4,28},{... | collective-permute-start | bytes 196616 | tf_op jit(solution)/shard_map/ppermute | solution.py:12
  812.9 8.2 collective-permute-start.2
  821.1 7.5 collective-permute-start.3
  828.6 6.9 collective-permute-start.4
  835.5 6.6 collective-permute-start.5
  842.1 6.0 collective-permute-start.6
  848.1 2.2 collective-permute-start.7
  850.3 4.5 collective-permute-start.8
  854.8 4.6 collective-permute-start.9
  872.3 68.8 %copy-start.12 = (f32[2048]{0:T(1024)S(1)}, f32[2048]{0:T(1024)}, u32[]{:S(2)}) copy-start(f32[2048]{0:T(1024)} %param.14) | copy-start | bytes 24580
Sparse Core Ops, SparseCore 0:
  874.2 62.1 all-gather.2
